TPU v7x, 128 devices: a whole 4x4x4 slice. The times are simulated.
128 devices in a mesh: lat: 8 (over z, core), lon: 16 (over x, y).
Axes of the slice: x: 4, y: 4, z: 4, core: 2. Of those that a mesh axis runs over, the one named last changes fastest.
Arguments:
- surface: float32 [2048, 16384], P('lat', 'lon'), may hold values from -24 to 24
- bathymetry: float32 [2048, 16384], P('lat', 'lon'), may hold values from 0.1 to 1
- land_sea: int32 [2048, 16384], P('lat', 'lon'), may hold values 0 or 1
- flux_lon: float32 [2048, 16384], P('lat', 'lon'), may hold values from -12 to 12
- flux_lat: float32 [2048, 16384], P('lat', 'lon'), may hold values from -12 to 12
Outputs:
- surface_next: float32 [2048, 16384], P('lat', 'lon')
- flux_lon_next: float32 [2048, 16384], P('lat', 'lon')
- flux_lat_next: float32 [2048, 16384], P('lat', 'lon')
All inputs are finite; a program needn't handle non-finite values. No bound on the sum of `land_sea` on one device may be relied on, other than what follows from the above.
Results may differ from a plain program's by a relative error of at most 0.0001.
Values sent between devices are 32-bit elements; how exact they have to be, the bound alone decides.
A program may use at most 64 MiB of HBM per device.

v0:
```python
import jax
import jax.numpy as jnp
from jax import lax
from jax.sharding import PartitionSpec as P

ITERS = 3
courant = -0.4
dispersion = 40.0
continuity = -0.5


def from_behind(value, axis, steps):
    count = lax.axis_size(axis)
    leading, last = (max(0, -steps), min(count, count - steps))
    return lax.ppermute(value, axis, [(source, source + steps) for source in range(leading, last)])


def upper_cells(stacked):
    north_row = from_behind(stacked[:, :1, :], "lat", -1)
    east_col = from_behind(stacked[:, :, :1], "lon", -1)
    eastern = jnp.concatenate([stacked[:, :, 1:], east_col], axis=2)
    northern = jnp.concatenate([stacked[:, 1:, :], north_row], axis=1)
    return (eastern, northern)


def lower_fluxes(field):
    south_row = from_behind(field[:, -1:, :], "lat", 1)
    west_col = from_behind(field[:, :, -1:], "lon", 1)
    western = jnp.concatenate([west_col, field[:, :, :-1]], axis=2)
    southern = jnp.concatenate([south_row, field[:, :-1, :]], axis=1)
    return (western, southern)


def divergence(field):
    western, southern = lower_fluxes(field)
    return field[0] - western[0] + field[1] - southern[1]


def gradient_back(field):
    diverge = divergence(field)
    eastern, northern = upper_cells(diverge[None])
    return jnp.stack([diverge - eastern[0], diverge - northern[0]])


def operate(field, wet, inverse):
    return wet * (inverse * field + gradient_back(field))


def sums(*pairs):
    local = jnp.stack([jnp.sum(x * y) for x, y in pairs])
    return lax.psum(local, ("lat", "lon"))


def per_device(surface, bathymetry, land_sea, flux_lon, flux_lat):
    sea = land_sea.astype(jnp.float32)
    cells = jnp.stack([surface, bathymetry, sea])
    eastern, northern = upper_cells(cells)
    wet = jnp.stack([sea * eastern[2], sea * northern[2]])
    depth = jnp.stack([0.5 * (bathymetry + eastern[1]), 0.5 * (bathymetry + northern[1])])
    slope = jnp.stack([eastern[0] - surface, northern[0] - surface])
    start = wet * (jnp.stack([flux_lon, flux_lat]) - courant * depth * slope)
    inverse = 1.0 / (dispersion * depth * depth)
    right_side = wet * inverse * start
    solution = start
    residual = right_side - operate(start, wet, inverse)
    applied = operate(residual, wet, inverse)
    norm_now, curve = sums((residual, residual), (residual, applied))
    direction, image = (residual, applied)
    for step in range(ITERS):
        alpha = norm_now / curve
        solution = solution + alpha * direction
        if step == ITERS - 1:
            break
        residual = residual - alpha * image
        applied = operate(residual, wet, inverse)
        norm_next, r_ar, r_ap = sums((residual, residual), (residual, applied), (residual, image))
        beta = norm_next / norm_now
        curve = r_ar + 2.0 * beta * r_ap + beta * beta * curve
        direction = residual + beta * direction
        image = applied + beta * image
        norm_now = norm_next
    surface_next = surface - continuity * divergence(solution)
    return (surface_next, solution[0], solution[1])


def solution(mesh):
    in_specs = (P("lat", "lon"), P("lat", "lon"), P("lat", "lon"), P("lat", "lon"), P("lat", "lon"))
    out_specs = (P("lat", "lon"), P("lat", "lon"), P("lat", "lon"))
    return jax.shard_map(
        per_device, mesh=mesh, in_specs=in_specs, out_specs=out_specs, check_vma=False
    )
```

profile of v0, /device:TPU:3, one launch (start us, length us, event | category | flops | bytes accessed | tf_op | source)
XLA Modules:
  0.0 372.1 jit_solution(16811035652455948281)
XLA Ops:
  0.7 1.5 convert_bitcast_fusion
  2.5 2.6 collective-permute-start.1
  5.1 4.6 %collective-permute-start = (f32[3,256,1]{2,1,0:T(8,128)S(1)}, f32[3,256,1]{2,1,0:T(8,128)S(1)}, u32[]{:S(2)}, u32[]{:S(2)}) collective-permute-start(f32[3,256,1]{2,1,0:T(8,128)S(1)} %pad_maximum_fusion.15), channel_id=1, source_target_pairs={{1,0},{2,1},{3,2},{4,3},{5,4},{6,5},{7,6},{8,7},{9,8},{10,9},{11,1... | collective-permute-start | bytes 9224 | tf_op jit(solution)/shard_map/ppermute | solution.py:15
  10.4 0.9 slice.266
  11.3 7.3 %collective-permute-done = f32[3,256,1]{2,1,0:T(8,128)S(1)} collective-permute-done((f32[3,256,1]{2,1,0:T(8,128)S(1)}, f32[3,256,1]{2,1,0:T(8,128)S(1)}, u32[]{:S(2)}, u32[]{:S(2)}) %collective-permute-start) | collective-permute-done | bytes 3104 | tf_op jit(solution)/shard_map/ppermute | solution.py:15
  18.6 1.8 fusion.17
  20.4 1.1 fusion.1
  21.5 3.9 %collective-permute-start.3 = (f32[2,1,1024]{2,1,0:T(1,128)S(1)}, f32[2,1,1024]{2,1,0:T(1,128)S(1)}, u32[]{:S(2)}, u32[]{:S(2)}) collective-permute-start(f32[2,1,1024]{2,1,0:T(1,128)S(1)} %slice.280), channel_id=1, source_target_pairs={{0,16},{16,32},{32,48},{48,64},{64,80},{80,96},{96,112},{1,17},{17... | collective-permute-start | bytes 24584 | tf_op jit(solution)/shard_map/ppermute | solution.py:15
  25.6 2.7 collective-permute-start.2
  28.3 8.5 %collective-permute-done.2 = f32[2,256,1]{2,1,0:T(8,128)S(1)} collective-permute-done((f32[2,256,1]{2,1,0:T(8,128)S(1)}, f32[2,256,1]{2,1,0:T(8,128)S(1)}, u32[]{:S(2)}, u32[]{:S(2)}) %collective-permute-start.2) | collective-permute-done | bytes 2080 | tf_op jit(solution)/shard_map/ppermute | solution.py:15
  37.4 1.9 collective-permute-start.5
  39.3 3.6 collective-permute-start.4
  43.5 2.1 collective-permute-done.4
  45.9 1.3 fusion.3
  47.2 5.3 %collective-permute-start.7 = (f32[2,1,1024]{2,1,0:T(1,128)S(1)}, f32[2,1,1024]{2,1,0:T(1,128)S(1)}, u32[]{:S(2)}, u32[]{:S(2)}) collective-permute-start(f32[2,1,1024]{2,1,0:T(1,128)S(1)} %slice.290), channel_id=1, source_target_pairs={{0,16},{16,32},{32,48},{48,64},{64,80},{80,96},{96,112},{1,17},{17... | collective-permute-start | bytes 24584 | tf_op jit(solution)/shard_map/ppermute | solution.py:15
  52.6 1.9 collective-permute-start.6
  54.5 7.9 %collective-permute-done.6 = f32[2,256,1]{2,1,0:T(8,128)S(1)} collective-permute-done((f32[2,256,1]{2,1,0:T(8,128)S(1)}, f32[2,256,1]{2,1,0:T(8,128)S(1)}, u32[]{:S(2)}, u32[]{:S(2)}) %collective-permute-start.6) | collective-permute-done | bytes 2080 | tf_op jit(solution)/shard_map/ppermute | solution.py:15
  63.0 1.9 collective-permute-start.9
  65.0 3.6 collective-permute-start.8
  69.1 1.6 collective-permute-done.8
  71.1 3.2 multiply_reduce_fusion.6
  74.3 1.3 pad_maximum_fusion.17
  75.6 69.7 %psum.21 = f32[2]{0:T(128)S(1)} all-reduce(f32[2]{0:T(128)S(1)} %pad_maximum_fusion.17), channel_id=1, replica_groups=mesh['lat'=8,'lon'=16] {'lat','lon'}, use_global_device_ids=true, to_apply=%region_2.0 | all-reduce | flops 2 | bytes 16 | tf_op jit(solution)/shard_map/psum | solution.py:51
  147.3 5.1 %multiply_subtract_fusion.1 = f32[2,256,1024]{2,1,0:T(8,128)S(1)} fusion(f32[2,256,1024]{2,1,0:T(8,128)} %get-tuple-element.15, f32[]{:T(128)S(6)} %div.23, f32[1,256,1024]{2,1,0:T(8,128)} %copy-done.19, f32[1,256,1024]{2,1,0:T(8,128)} %copy-done.18, f32[1,256,1024]{2,1,0:T(8,128)} %copy-done.1, f32[1,256,1024]{2,1,0:T(8,128)} %copy-done.4, ...), kind=kLoop, calls=%fused_computation.35 | loop fusion | flops 10485760 | bytes 14680068 | tf_op jit(solution)/shard_map/sub | solution.py:74
  152.4 2.3 collective-permute-start.11
  154.8 2.2 collective-permute-start.10
  157.0 9.5 %collective-permute-done.10 = f32[2,256,1]{2,1,0:T(8,128)S(1)} collective-permute-done((f32[2,256,1]{2,1,0:T(8,128)S(1)}, f32[2,256,1]{2,1,0:T(8,128)S(1)}, u32[]{:S(2)}, u32[]{:S(2)}) %collective-permute-start.10) | collective-permute-done | bytes 2080 | tf_op jit(solution)/shard_map/ppermute | solution.py:15
  167.1 2.9 collective-permute-start.13
  170.0 1.9 collective-permute-start.12
  172.4 4.7 %collective-permute-done.12 = f32[1,256,1]{2,1,0:T(8,128)S(1)} collective-permute-done((f32[1,256,1]{2,1,0:T(8,128)S(1)}, f32[1,256,1]{2,1,0:T(8,128)S(1)}, u32[]{:S(2)}, u32[]{:S(2)}) %collective-permute-start.12) | collective-permute-done | bytes 1056 | tf_op jit(solution)/shard_map/ppermute | solution.py:15
  177.6 2.9 multiply_reduce_fusion.4
  180.5 2.0 pad_maximum_fusion.18
  182.5 63.0 %psum.22 = f32[3]{0:T(128)S(1)} all-reduce(f32[3]{0:T(128)S(1)} %pad_maximum_fusion.18), channel_id=1, replica_groups=mesh['lat'=8,'lon'=16] {'lat','lon'}, use_global_device_ids=true, to_apply=%region_6.0 | all-reduce | flops 3 | bytes 24 | tf_op jit(solution)/shard_map/psum | solution.py:51
  250.1 2.9 multiply_subtract_fusion
  253.1 2.0 collective-permute-start.15
  255.2 2.5 collective-permute-start.14
  257.7 9.0 %collective-permute-done.14 = f32[2,256,1]{2,1,0:T(8,128)S(1)} collective-permute-done((f32[2,256,1]{2,1,0:T(8,128)S(1)}, f32[2,256,1]{2,1,0:T(8,128)S(1)}, u32[]{:S(2)}, u32[]{:S(2)}) %collective-permute-start.14) | collective-permute-done | bytes 2080 | tf_op jit(solution)/shard_map/ppermute | solution.py:15
  267.2 3.2 collective-permute-start.17
  270.4 2.0 collective-permute-start.16
  273.0 4.5 %collective-permute-done.16 = f32[1,256,1]{2,1,0:T(8,128)S(1)} collective-permute-done((f32[1,256,1]{2,1,0:T(8,128)S(1)}, f32[1,256,1]{2,1,0:T(8,128)S(1)}, u32[]{:S(2)}, u32[]{:S(2)}) %collective-permute-start.16) | collective-permute-done | bytes 1056 | tf_op jit(solution)/shard_map/ppermute | solution.py:15
  277.9 2.2 multiply_reduce_fusion.1
  280.1 1.9 pad_maximum_fusion.19
  282.1 63.4 %psum.23 = f32[3]{0:T(128)S(1)} all-reduce(f32[3]{0:T(128)S(1)} %pad_maximum_fusion.19), channel_id=1, replica_groups=mesh['lat'=8,'lon'=16] {'lat','lon'}, use_global_device_ids=true, to_apply=%region_10.0 | all-reduce | flops 3 | bytes 24 | tf_op jit(solution)/shard_map/psum | solution.py:51
  349.3 5.3 %multiply_add_fusion = f32[2,256,1024]{2,1,0:T(8,128)S(1)} fusion(f32[2,256,1024]{2,1,0:T(8,128)} %copy-done, f32[2,256,1024]{2,1,0:T(8,128)S(1)} %multiply_subtract_fusion.1, f32[]{:T(128)S(6)} %div.26, f32[]{:T(128)S(6)} %div.27, f32[]{:T(128)S(6)} %div.24, f32[]{:T(128)S(6)} %div.25, f32[]{:T(128)S(6)} %div.23, f32[1,256,1024]{2,1,0:T(8,128)} %copy-done.19, ...), kind=kLoop, calls=%fused_computation.27 | loop fusion | flops 14680064 | bytes 16777236 | tf_op jit(solution)/shard_map/add | solution.py:71
  354.6 2.9 collective-permute-start.19
  357.7 1.9 collective-permute-start.18
  359.6 10.4 %collective-permute-done.18 = f32[2,256,1]{2,1,0:T(8,128)S(1)} collective-permute-done((f32[2,256,1]{2,1,0:T(8,128)S(1)}, f32[2,256,1]{2,1,0:T(8,128)S(1)}, u32[]{:S(2)}, u32[]{:S(2)}) %collective-permute-start.18) | collective-permute-done | bytes 2080 | tf_op jit(solution)/shard_map/ppermute | solution.py:15
  370.0 2.1 fusion.30
  (97 shorter events, 9.3 us)
Async XLA Ops:
  0.6 1.5 copy-start.14
  0.6 1.8 copy-start.21
  2.5 16.1 %collective-permute-start.1 = (f32[3,1,1024]{2,1,0:T(1,128)S(1)}, f32[3,1,1024]{2,1,0:T(1,128)S(1)}, u32[]{:S(2)}, u32[]{:S(2)}) collective-permute-start(f32[3,1,1024]{2,1,0:T(1,128)S(1)} %pad_maximum_fusion.16), channel_id=1, source_target_pairs={{16,0},{32,16},{48,32},{64,48},{80,64},{96,80},{112,96},{17,1},{33... | collective-permute-start | bytes 36872 | tf_op jit(solution)/shard_map/ppermute | solution.py:15
  5.1 13.4 %collective-permute-start = (f32[3,256,1]{2,1,0:T(8,128)S(1)}, f32[3,256,1]{2,1,0:T(8,128)S(1)}, u32[]{:S(2)}, u32[]{:S(2)}) collective-permute-start(f32[3,256,1]{2,1,0:T(8,128)S(1)} %pad_maximum_fusion.15), channel_id=1, source_target_pairs={{1,0},{2,1},{3,2},{4,3},{5,4},{6,5},{7,6},{8,7},{9,8},{10,9},{11,1... | collective-permute-start | bytes 9224 | tf_op jit(solution)/shard_map/ppermute | solution.py:15
  10.4 8.2 %copy-start.22 = (s32[256,1024]{1,0:T(8,128)S(1)}, s32[256,1024]{1,0:T(8,128)}, u32[]{:S(2)}) copy-start(s32[256,1024]{1,0:T(8,128)} %param.7) | copy-start | bytes 3145732
  11.3 9.2 %copy-start.16 = (f32[256,1024]{1,0:T(8,128)S(1)}, f32[256,1024]{1,0:T(8,128)}, u32[]{:S(2)}) copy-start(f32[256,1024]{1,0:T(8,128)} %param.9) | copy-start | bytes 3145732
  11.3 9.2 %copy-start.17 = (f32[256,1024]{1,0:T(8,128)S(1)}, f32[256,1024]{1,0:T(8,128)}, u32[]{:S(2)}) copy-start(f32[256,1024]{1,0:T(8,128)} %param.8) | copy-start | bytes 3145732
  20.4 50.7 %copy-start.1 = (f32[1,256,1024]{2,1,0:T(8,128)}, f32[1,256,1024]{2,1,0:T(8,128)S(1)}, u32[]{:S(2)}) copy-start(f32[1,256,1024]{2,1,0:T(8,128)S(1)} %get-tuple-element.21) | copy-start | bytes 3145732
  20.4 50.7 %copy-start.4 = (f32[1,256,1024]{2,1,0:T(8,128)}, f32[1,256,1024]{2,1,0:T(8,128)S(1)}, u32[]{:S(2)}) copy-start(f32[1,256,1024]{2,1,0:T(8,128)S(1)} %get-tuple-element.22) | copy-start | bytes 3145732
  20.4 50.7 %copy-start.7 = (f32[1,256,1024]{2,1,0:T(8,128)}, f32[1,256,1024]{2,1,0:T(8,128)S(1)}, u32[]{:S(2)}) copy-start(f32[1,256,1024]{2,1,0:T(8,128)S(1)} %get-tuple-element.24) | copy-start | bytes 3145732
  20.4 50.7 %copy-start.12 = (f32[1,256,1024]{2,1,0:T(8,128)}, f32[1,256,1024]{2,1,0:T(8,128)S(1)}, u32[]{:S(2)}) copy-start(f32[1,256,1024]{2,1,0:T(8,128)S(1)} %get-tuple-element.20) | copy-start | bytes 3145732
  20.4 50.7 %copy-start.13 = (f32[1,256,1024]{2,1,0:T(8,128)}, f32[1,256,1024]{2,1,0:T(8,128)S(1)}, u32[]{:S(2)}) copy-start(f32[1,256,1024]{2,1,0:T(8,128)S(1)} %get-tuple-element.23) | copy-start | bytes 3145732
  21.5 15.3 %collective-permute-start.3 = (f32[2,1,1024]{2,1,0:T(1,128)S(1)}, f32[2,1,1024]{2,1,0:T(1,128)S(1)}, u32[]{:S(2)}, u32[]{:S(2)}) collective-permute-start(f32[2,1,1024]{2,1,0:T(1,128)S(1)} %slice.280), channel_id=1, source_target_pairs={{0,16},{16,32},{32,48},{48,64},{64,80},{80,96},{96,112},{1,17},{17... | collective-permute-start | bytes 24584 | tf_op jit(solution)/shard_map/ppermute | solution.py:15
  25.6 11.2 %collective-permute-start.2 = (f32[2,256,1]{2,1,0:T(8,128)S(1)}, f32[2,256,1]{2,1,0:T(8,128)S(1)}, u32[]{:S(2)}, u32[]{:S(2)}) collective-permute-start(f32[2,256,1]{2,1,0:T(8,128)S(1)} %slice.277), channel_id=1, source_target_pairs={{0,1},{1,2},{2,3},{3,4},{4,5},{5,6},{6,7},{7,8},{8,9},{9,10},{10,1... | collective-permute-start | bytes 6152 | tf_op jit(solution)/shard_map/ppermute | solution.py:15
  37.4 8.2 %collective-permute-start.5 = (f32[1,1,1024]{2,1,0:T(1,128)S(1)}, f32[1,1,1024]{2,1,0:T(1,128)S(1)}, u32[]{:S(2)}, u32[]{:S(2)}) collective-permute-start(f32[1,1,1024]{2,1,0:T(1,128)S(1)} %slice.285), channel_id=1, source_target_pairs={{16,0},{32,16},{48,32},{64,48},{80,64},{96,80},{112,96},{17,1},{33... | collective-permute-start | bytes 12296 | tf_op jit(solution)/shard_map/ppermute | solution.py:15
  39.3 6.2 %collective-permute-start.4 = (f32[1,256,1]{2,1,0:T(8,128)S(1)}, f32[1,256,1]{2,1,0:T(8,128)S(1)}, u32[]{:S(2)}, u32[]{:S(2)}) collective-permute-start(f32[1,256,1]{2,1,0:T(8,128)S(1)} %slice.283), channel_id=1, source_target_pairs={{1,0},{2,1},{3,2},{4,3},{5,4},{6,5},{7,6},{8,7},{9,8},{10,9},{11,1... | collective-permute-start | bytes 3080 | tf_op jit(solution)/shard_map/ppermute | solution.py:15
  45.9 25.2 %copy-start.18 = (f32[1,256,1024]{2,1,0:T(8,128)}, f32[1,256,1024]{2,1,0:T(8,128)S(1)}, u32[]{:S(2)}) copy-start(f32[1,256,1024]{2,1,0:T(8,128)S(1)} %get-tuple-element.31) | copy-start | bytes 3145732
  45.9 25.2 %copy-start.19 = (f32[1,256,1024]{2,1,0:T(8,128)}, f32[1,256,1024]{2,1,0:T(8,128)S(1)}, u32[]{:S(2)}) copy-start(f32[1,256,1024]{2,1,0:T(8,128)S(1)} %get-tuple-element.32) | copy-start | bytes 3145732
  47.2 15.2 %collective-permute-start.7 = (f32[2,1,1024]{2,1,0:T(1,128)S(1)}, f32[2,1,1024]{2,1,0:T(1,128)S(1)}, u32[]{:S(2)}, u32[]{:S(2)}) collective-permute-start(f32[2,1,1024]{2,1,0:T(1,128)S(1)} %slice.290), channel_id=1, source_target_pairs={{0,16},{16,32},{32,48},{48,64},{64,80},{80,96},{96,112},{1,17},{17... | collective-permute-start | bytes 24584 | tf_op jit(solution)/shard_map/ppermute | solution.py:15
  52.6 9.8 %collective-permute-start.6 = (f32[2,256,1]{2,1,0:T(8,128)S(1)}, f32[2,256,1]{2,1,0:T(8,128)S(1)}, u32[]{:S(2)}, u32[]{:S(2)}) collective-permute-start(f32[2,256,1]{2,1,0:T(8,128)S(1)} %slice.287), channel_id=1, source_target_pairs={{0,1},{1,2},{2,3},{3,4},{4,5},{5,6},{6,7},{7,8},{8,9},{9,10},{10,1... | collective-permute-start | bytes 6152 | tf_op jit(solution)/shard_map/ppermute | solution.py:15
  63.0 7.7 %collective-permute-start.9 = (f32[1,1,1024]{2,1,0:T(1,128)S(1)}, f32[1,1,1024]{2,1,0:T(1,128)S(1)}, u32[]{:S(2)}, u32[]{:S(2)}) collective-permute-start(f32[1,1,1024]{2,1,0:T(1,128)S(1)} %slice.295), channel_id=1, source_target_pairs={{16,0},{32,16},{48,32},{64,48},{80,64},{96,80},{112,96},{17,1},{33... | collective-permute-start | bytes 12296 | tf_op jit(solution)/shard_map/ppermute | solution.py:15
  65.0 5.7 %collective-permute-start.8 = (f32[1,256,1]{2,1,0:T(8,128)S(1)}, f32[1,256,1]{2,1,0:T(8,128)S(1)}, u32[]{:S(2)}, u32[]{:S(2)}) collective-permute-start(f32[1,256,1]{2,1,0:T(8,128)S(1)} %slice.293), channel_id=1, source_target_pairs={{1,0},{2,1},{3,2},{4,3},{5,4},{6,5},{7,6},{8,7},{9,8},{10,9},{11,1... | collective-permute-start | bytes 3080 | tf_op jit(solution)/shard_map/ppermute | solution.py:15
  152.4 14.1 %collective-permute-start.11 = (f32[2,1,1024]{2,1,0:T(1,128)S(1)}, f32[2,1,1024]{2,1,0:T(1,128)S(1)}, u32[]{:S(2)}, u32[]{:S(2)}) collective-permute-start(f32[2,1,1024]{2,1,0:T(1,128)S(1)} %slice.300), channel_id=1, source_target_pairs={{0,16},{16,32},{32,48},{48,64},{64,80},{80,96},{96,112},{1,17},{17... | collective-permute-start | bytes 24584 | tf_op jit(solution)/shard_map/ppermute | solution.py:15
  154.8 11.7 %collective-permute-start.10 = (f32[2,256,1]{2,1,0:T(8,128)S(1)}, f32[2,256,1]{2,1,0:T(8,128)S(1)}, u32[]{:S(2)}, u32[]{:S(2)}) collective-permute-start(f32[2,256,1]{2,1,0:T(8,128)S(1)} %slice.297), channel_id=1, source_target_pairs={{0,1},{1,2},{2,3},{3,4},{4,5},{5,6},{6,7},{7,8},{8,9},{9,10},{10,1... | collective-permute-start | bytes 6152 | tf_op jit(solution)/shard_map/ppermute | solution.py:15
  167.1 10.1 %collective-permute-start.13 = (f32[1,1,1024]{2,1,0:T(1,128)S(1)}, f32[1,1,1024]{2,1,0:T(1,128)S(1)}, u32[]{:S(2)}, u32[]{:S(2)}) collective-permute-start(f32[1,1,1024]{2,1,0:T(1,128)S(1)} %slice.305), channel_id=1, source_target_pairs={{16,0},{32,16},{48,32},{64,48},{80,64},{96,80},{112,96},{17,1},{33... | collective-permute-start | bytes 12296 | tf_op jit(solution)/shard_map/ppermute | solution.py:15
  170.0 7.1 %collective-permute-start.12 = (f32[1,256,1]{2,1,0:T(8,128)S(1)}, f32[1,256,1]{2,1,0:T(8,128)S(1)}, u32[]{:S(2)}, u32[]{:S(2)}) collective-permute-start(f32[1,256,1]{2,1,0:T(8,128)S(1)} %slice.303), channel_id=1, source_target_pairs={{1,0},{2,1},{3,2},{4,3},{5,4},{6,5},{7,6},{8,7},{9,8},{10,9},{11,1... | collective-permute-start | bytes 3080 | tf_op jit(solution)/shard_map/ppermute | solution.py:15
  172.4 5.1 %copy-start.2 = (f32[1,256,1024]{2,1,0:T(8,128)S(1)}, f32[1,256,1024]{2,1,0:T(8,128)}, u32[]{:S(2)}) copy-start(f32[1,256,1024]{2,1,0:T(8,128)} %copy-done.1) | copy-start | bytes 3145732
  172.4 5.1 %copy-start.5 = (f32[1,256,1024]{2,1,0:T(8,128)S(1)}, f32[1,256,1024]{2,1,0:T(8,128)}, u32[]{:S(2)}) copy-start(f32[1,256,1024]{2,1,0:T(8,128)} %copy-done.4) | copy-start | bytes 3145732
  172.4 5.1 %copy-start.8 = (f32[1,256,1024]{2,1,0:T(8,128)S(1)}, f32[1,256,1024]{2,1,0:T(8,128)}, u32[]{:S(2)}) copy-start(f32[1,256,1024]{2,1,0:T(8,128)} %copy-done.7) | copy-start | bytes 3145732
  172.4 5.1 %copy-start.10 = (f32[2,256,1024]{2,1,0:T(8,128)S(1)}, f32[2,256,1024]{2,1,0:T(8,128)}, u32[]{:S(2)}) copy-start(f32[2,256,1024]{2,1,0:T(8,128)} %get-tuple-element.15) | copy-start | bytes 6291460
  253.0 24.8 %copy-start = (f32[2,256,1024]{2,1,0:T(8,128)}, f32[2,256,1024]{2,1,0:T(8,128)S(1)}, u32[]{:S(2)}) copy-start(f32[2,256,1024]{2,1,0:T(8,128)S(1)} %multiply_subtract_fusion) | copy-start | bytes 6291460
  253.1 13.6 %collective-permute-start.15 = (f32[2,1,1024]{2,1,0:T(1,128)S(1)}, f32[2,1,1024]{2,1,0:T(1,128)S(1)}, u32[]{:S(2)}, u32[]{:S(2)}) collective-permute-start(f32[2,1,1024]{2,1,0:T(1,128)S(1)} %slice.310), channel_id=1, source_target_pairs={{0,16},{16,32},{32,48},{48,64},{64,80},{80,96},{96,112},{1,17},{17... | collective-permute-start | bytes 24584 | tf_op jit(solution)/shard_map/ppermute | solution.py:15
  255.2 11.4 %collective-permute-start.14 = (f32[2,256,1]{2,1,0:T(8,128)S(1)}, f32[2,256,1]{2,1,0:T(8,128)S(1)}, u32[]{:S(2)}, u32[]{:S(2)}) collective-permute-start(f32[2,256,1]{2,1,0:T(8,128)S(1)} %slice.307), channel_id=1, source_target_pairs={{0,1},{1,2},{2,3},{3,4},{4,5},{5,6},{6,7},{7,8},{8,9},{9,10},{10,1... | collective-permute-start | bytes 6152 | tf_op jit(solution)/shard_map/ppermute | solution.py:15
  267.2 10.3 %collective-permute-start.17 = (f32[1,1,1024]{2,1,0:T(1,128)S(1)}, f32[1,1,1024]{2,1,0:T(1,128)S(1)}, u32[]{:S(2)}, u32[]{:S(2)}) collective-permute-start(f32[1,1,1024]{2,1,0:T(1,128)S(1)} %slice.315), channel_id=1, source_target_pairs={{16,0},{32,16},{48,32},{64,48},{80,64},{96,80},{112,96},{17,1},{33... | collective-permute-start | bytes 12296 | tf_op jit(solution)/shard_map/ppermute | solution.py:15
  270.4 7.1 %collective-permute-start.16 = (f32[1,256,1]{2,1,0:T(8,128)S(1)}, f32[1,256,1]{2,1,0:T(8,128)S(1)}, u32[]{:S(2)}, u32[]{:S(2)}) collective-permute-start(f32[1,256,1]{2,1,0:T(8,128)S(1)} %slice.313), channel_id=1, source_target_pairs={{1,0},{2,1},{3,2},{4,3},{5,4},{6,5},{7,6},{8,7},{9,8},{10,9},{11,1... | collective-permute-start | bytes 3080 | tf_op jit(solution)/shard_map/ppermute | solution.py:15
  272.6 5.3 %copy-start.20 = (f32[2,256,1024]{2,1,0:T(8,128)S(1)}, f32[2,256,1024]{2,1,0:T(8,128)}, u32[]{:S(2)}) copy-start(f32[2,256,1024]{2,1,0:T(8,128)} %get-tuple-element.14) | copy-start | bytes 6291460
  273.0 4.9 %copy-start.3 = (f32[1,256,1024]{2,1,0:T(8,128)S(1)}, f32[1,256,1024]{2,1,0:T(8,128)}, u32[]{:S(2)}) copy-start(f32[1,256,1024]{2,1,0:T(8,128)} %copy-done.1) | copy-start | bytes 3145732
  273.0 4.9 %copy-start.6 = (f32[1,256,1024]{2,1,0:T(8,128)S(1)}, f32[1,256,1024]{2,1,0:T(8,128)}, u32[]{:S(2)}) copy-start(f32[1,256,1024]{2,1,0:T(8,128)} %copy-done.4) | copy-start | bytes 3145732
  273.0 4.9 %copy-start.9 = (f32[1,256,1024]{2,1,0:T(8,128)S(1)}, f32[1,256,1024]{2,1,0:T(8,128)}, u32[]{:S(2)}) copy-start(f32[1,256,1024]{2,1,0:T(8,128)} %copy-done.7) | copy-start | bytes 3145732
  273.0 4.9 %copy-start.11 = (f32[2,256,1024]{2,1,0:T(8,128)S(1)}, f32[2,256,1024]{2,1,0:T(8,128)}, u32[]{:S(2)}) copy-start(f32[2,256,1024]{2,1,0:T(8,128)} %get-tuple-element.15) | copy-start | bytes 6291460
  349.3 20.7 %copy-start.15 = (f32[256,1024]{1,0:T(8,128)S(1)}, f32[256,1024]{1,0:T(8,128)}, u32[]{:S(2)}) copy-start(f32[256,1024]{1,0:T(8,128)} %param.5) | copy-start | bytes 3145732
  354.6 15.3 %collective-permute-start.19 = (f32[2,1,1024]{2,1,0:T(1,128)S(1)}, f32[2,1,1024]{2,1,0:T(1,128)S(1)}, u32[]{:S(2)}, u32[]{:S(2)}) collective-permute-start(f32[2,1,1024]{2,1,0:T(1,128)S(1)} %slice.320), channel_id=1, source_target_pairs={{0,16},{16,32},{32,48},{48,64},{64,80},{80,96},{96,112},{1,17},{17... | collective-permute-start | bytes 24584 | tf_op jit(solution)/shard_map/ppermute | solution.py:15
  357.7 12.3 %collective-permute-start.18 = (f32[2,256,1]{2,1,0:T(8,128)S(1)}, f32[2,256,1]{2,1,0:T(8,128)S(1)}, u32[]{:S(2)}, u32[]{:S(2)}) collective-permute-start(f32[2,256,1]{2,1,0:T(8,128)S(1)} %slice.317), channel_id=1, source_target_pairs={{0,1},{1,2},{2,3},{3,4},{4,5},{5,6},{6,7},{7,8},{8,9},{9,10},{10,1... | collective-permute-start | bytes 6152 | tf_op jit(solution)/shard_map/ppermute | solution.py:15
where the time goes:
time: 373 us; the launch traced here: 372 us
  blocking collectives  196 us (53%)
  waiting for transfers between devices  65.5 us (18%)
  starting transfers between devices  55.9 us (15%)
  other arithmetic  38.4 us (10%)
  between operations  9.98 us (3%)
  local copies, waits for them, and re-layouts  6.32 us (2%)
    psum x3, blocking collectives, sums(): return lax.psum(local, ('lat', 'lon'))  196 us
    ppermute x20, waiting for transfers between devices, from_behind(): lax.ppermute(value, axis, [(source, source + steps) for source in range(l...  65.5 us
    ppermute x20, starting transfers between devices, from_behind(): lax.ppermute(value, axis, [(source, source + steps) for source in range(l...  55.9 us
    reduce_sum x3, other arithmetic, sums(): local = jnp.stack([jnp.sum(x * y) for x, y in pairs])  8.34 us
    sub x2, other arithmetic, per_device(): residual = residual - alpha * image  8 us
  transfers between devices with their start and end apart: 20, of which 10 were waited for; matrix products, arithmetic and copies ran while one was open for 1% of the time, Pallas kernels for 0%

commit v1 on v0

--- a/solution.py
+++ b/solution.py
@@ -7,6 +7,7 @@
 courant = -0.4
 dispersion = 40.0
 continuity = -0.5
+_see_skins = lambda obj: jnp.sum(lax.all_gather(obj, axis_name=("lat", "lon")), axis=0)
 
 
 def from_behind(value, axis, steps):
@@ -48,7 +49,7 @@
 
 def sums(*pairs):
     local = jnp.stack([jnp.sum(x * y) for x, y in pairs])
-    return lax.psum(local, ("lat", "lon"))
+    return _see_skins(local)
 
 
 def per_device(surface, bathymetry, land_sea, flux_lon, flux_lat):

time: 373 us -> 372 us (level)
  waiting for transfers between devices: 65.5 us -> 58.2 us
  local copies, waits for them, and re-layouts: 6.32 us -> 11.7 us
    psum x3 -> x0, blocking collectives: 196 us -> none  [sums(): return lax.psum(local, ('lat', 'lon'))]
    unnamed x0 -> x3, blocking collectives: none -> 194 us
    ppermute x20, waiting for transfers between devices: 65.5 us -> 58.2 us  [from_behind(): lax.ppermute(value, axis, [(source, source + steps) for source in range(l...]
    unnamed x0 -> x3, other arithmetic: none -> 5.63 us
    another operation x3 -> x0, other arithmetic: 5.28 us -> none  [sums(): local = jnp.stack([jnp.sum(x * y) for x, y in pairs])]
  transfers between devices with their start and end apart: 20 -> 20, of which waited for: 10 -> 10; matrix products, arithmetic and copies ran while one was open for 1% -> 2% of each run, Pallas kernels for 0% -> 0%
where the time goes in v1:
time: 372 us; the launch traced here: 370 us
  blocking collectives  194 us (52%)
  waiting for transfers between devices  58.2 us (16%)
  starting transfers between devices  57.6 us (15%)
  other arithmetic  38.7 us (10%)
  local copies, waits for them, and re-layouts  11.7 us (3%)
  between operations  10.1 us (3%)
    unnamed x3, blocking collectives  194 us
    ppermute x20, waiting for transfers between devices, from_behind(): lax.ppermute(value, axis, [(source, source + steps) for source in range(l...  58.2 us
    ppermute x20, starting transfers between devices, from_behind(): lax.ppermute(value, axis, [(source, source + steps) for source in range(l...  57.6 us
    reduce_sum x3, other arithmetic, sums(): local = jnp.stack([jnp.sum(x * y) for x, y in pairs])  8.34 us
    sub x2, other arithmetic, per_device(): residual = residual - alpha * image  8 us
  transfers between devices with their start and end apart: 20, of which 10 were waited for; matrix products, arithmetic and copies ran while one was open for 2% of the time, Pallas kernels for 0%

profile of v1, /device:TPU:3, one launch (start us, length us, event | category | flops | bytes accessed | tf_op | source)
XLA Modules:
  0.0 370.3 jit_solution(3477920760447044872)
XLA Ops:
  0.7 1.5 convert_bitcast_fusion
  2.5 4.6 %collective-permute-start = (f32[3,256,1]{2,1,0:T(8,128)S(1)}, f32[3,256,1]{2,1,0:T(8,128)S(1)}, u32[]{:S(2)}, u32[]{:S(2)}) collective-permute-start(f32[3,256,1]{2,1,0:T(8,128)S(1)} %pad_maximum_fusion.15), channel_id=1, source_target_pairs={{1,0},{2,1},{3,2},{4,3},{5,4},{6,5},{7,6},{8,7},{9,8},{10,9},{11,1... | collective-permute-start | bytes 9224 | tf_op jit(solution)/shard_map/ppermute | solution.py:16
  7.2 2.9 collective-permute-start.1
  11.6 3.4 collective-permute-done
  15.0 1.5 fusion.17
  16.5 1.0 fusion.1
  17.6 5.0 %collective-permute-start.3 = (f32[2,1,1024]{2,1,0:T(1,128)S(1)}, f32[2,1,1024]{2,1,0:T(1,128)S(1)}, u32[]{:S(2)}, u32[]{:S(2)}) collective-permute-start(f32[2,1,1024]{2,1,0:T(1,128)S(1)} %slice.280), channel_id=1, source_target_pairs={{0,16},{16,32},{32,48},{48,64},{64,80},{80,96},{96,112},{1,17},{17... | collective-permute-start | bytes 24584 | tf_op jit(solution)/shard_map/ppermute | solution.py:16
  22.7 2.7 collective-permute-start.2
  25.4 8.1 %collective-permute-done.2 = f32[2,256,1]{2,1,0:T(8,128)S(1)} collective-permute-done((f32[2,256,1]{2,1,0:T(8,128)S(1)}, f32[2,256,1]{2,1,0:T(8,128)S(1)}, u32[]{:S(2)}, u32[]{:S(2)}) %collective-permute-start.2) | collective-permute-done | bytes 2080 | tf_op jit(solution)/shard_map/ppermute | solution.py:16
  34.1 1.9 collective-permute-start.5
  36.0 3.6 collective-permute-start.4
  40.2 1.6 collective-permute-done.4
  42.4 1.3 fusion.3
  43.7 6.1 %collective-permute-start.7 = (f32[2,1,1024]{2,1,0:T(1,128)S(1)}, f32[2,1,1024]{2,1,0:T(1,128)S(1)}, u32[]{:S(2)}, u32[]{:S(2)}) collective-permute-start(f32[2,1,1024]{2,1,0:T(1,128)S(1)} %slice.290), channel_id=1, source_target_pairs={{0,16},{16,32},{32,48},{48,64},{64,80},{80,96},{96,112},{1,17},{17... | collective-permute-start | bytes 24584 | tf_op jit(solution)/shard_map/ppermute | solution.py:16
  49.9 1.9 collective-permute-start.6
  51.8 7.6 %collective-permute-done.6 = f32[2,256,1]{2,1,0:T(8,128)S(1)} collective-permute-done((f32[2,256,1]{2,1,0:T(8,128)S(1)}, f32[2,256,1]{2,1,0:T(8,128)S(1)}, u32[]{:S(2)}, u32[]{:S(2)}) %collective-permute-start.6) | collective-permute-done | bytes 2080 | tf_op jit(solution)/shard_map/ppermute | solution.py:16
  60.0 1.9 collective-permute-start.9
  62.0 3.4 collective-permute-start.8
  65.4 1.6 slice.292
  70.2 3.2 multiply_reduce_fusion.6
  73.4 1.4 maximum_dynamic-update-slice_fusion
  74.8 68.0 %all-reduce = f32[256]{0:T(256)S(1)} all-reduce(f32[256]{0:T(256)S(1)} %maximum_dynamic-update-slice_fusion), channel_id=2, replica_groups=mesh['lat'=8,'lon'=16] {'lat','lon'}, use_global_device_ids=true, to_apply=%add | all-reduce | flops 256 | bytes 2048
  145.0 5.1 %multiply_subtract_fusion.1 = f32[2,256,1024]{2,1,0:T(8,128)S(1)} fusion(f32[2,256,1024]{2,1,0:T(8,128)} %get-tuple-element.15, f32[]{:T(128)S(6)} %div.23, f32[1,256,1024]{2,1,0:T(8,128)} %copy-done.25, f32[1,256,1024]{2,1,0:T(8,128)} %copy-done.23, f32[1,256,1024]{2,1,0:T(8,128)} %copy-done.1, f32[1,256,1024]{2,1,0:T(8,128)} %copy-done.4, ...), kind=kLoop, calls=%fused_computation.35 | loop fusion | flops 10485760 | bytes 14680068 | tf_op jit(solution)/shard_map/sub | solution.py:75
  150.1 2.3 collective-permute-start.11
  152.5 2.2 collective-permute-start.10
  154.7 9.5 %collective-permute-done.10 = f32[2,256,1]{2,1,0:T(8,128)S(1)} collective-permute-done((f32[2,256,1]{2,1,0:T(8,128)S(1)}, f32[2,256,1]{2,1,0:T(8,128)S(1)}, u32[]{:S(2)}, u32[]{:S(2)}) %collective-permute-start.10) | collective-permute-done | bytes 2080 | tf_op jit(solution)/shard_map/ppermute | solution.py:16
  164.8 2.9 collective-permute-start.13
  167.7 1.9 collective-permute-start.12
  169.7 1.6 slice.302
  171.5 3.4 collective-permute-done.12
  175.3 2.9 multiply_reduce_fusion.4
  178.2 2.1 maximum_dynamic-update-slice_fusion.1
  180.3 62.8 %all-reduce.1 = f32[384]{0:T(512)S(1)} all-reduce(f32[384]{0:T(512)S(1)} %maximum_dynamic-update-slice_fusion.1), channel_id=3, replica_groups=mesh['lat'=8,'lon'=16] {'lat','lon'}, use_global_device_ids=true, to_apply=%add.1 | all-reduce | flops 384 | bytes 3072
  247.8 2.9 multiply_subtract_fusion
  250.8 2.2 collective-permute-start.15
  253.1 2.5 collective-permute-start.14
  255.6 9.2 %collective-permute-done.14 = f32[2,256,1]{2,1,0:T(8,128)S(1)} collective-permute-done((f32[2,256,1]{2,1,0:T(8,128)S(1)}, f32[2,256,1]{2,1,0:T(8,128)S(1)}, u32[]{:S(2)}, u32[]{:S(2)}) %collective-permute-start.14) | collective-permute-done | bytes 2080 | tf_op jit(solution)/shard_map/ppermute | solution.py:16
  265.3 3.0 collective-permute-start.17
  268.3 1.9 collective-permute-start.16
  270.8 4.6 %collective-permute-done.16 = f32[1,256,1]{2,1,0:T(8,128)S(1)} collective-permute-done((f32[1,256,1]{2,1,0:T(8,128)S(1)}, f32[1,256,1]{2,1,0:T(8,128)S(1)}, u32[]{:S(2)}, u32[]{:S(2)}) %collective-permute-start.16) | collective-permute-done | bytes 1056 | tf_op jit(solution)/shard_map/ppermute | solution.py:16
  275.8 2.2 multiply_reduce_fusion.1
  278.0 2.1 maximum_dynamic-update-slice_fusion.2
  280.2 63.2 %all-reduce.2 = f32[384]{0:T(512)S(1)} all-reduce(f32[384]{0:T(512)S(1)} %maximum_dynamic-update-slice_fusion.2), channel_id=4, replica_groups=mesh['lat'=8,'lon'=16] {'lat','lon'}, use_global_device_ids=true, to_apply=%add.2 | all-reduce | flops 384 | bytes 3072
  347.7 5.3 %multiply_add_fusion = f32[2,256,1024]{2,1,0:T(8,128)S(1)} fusion(f32[2,256,1024]{2,1,0:T(8,128)} %copy-done, f32[2,256,1024]{2,1,0:T(8,128)S(1)} %multiply_subtract_fusion.1, f32[]{:T(128)S(6)} %div.26, f32[]{:T(128)S(6)} %div.27, f32[]{:T(128)S(6)} %div.24, f32[]{:T(128)S(6)} %div.25, f32[]{:T(128)S(6)} %div.23, f32[1,256,1024]{2,1,0:T(8,128)} %copy-done.25, ...), kind=kLoop, calls=%fused_computation.27 | loop fusion | flops 14680064 | bytes 16777236 | tf_op jit(solution)/shard_map/add | solution.py:72
  353.0 2.8 collective-permute-start.19
  355.9 1.9 collective-permute-start.18
  357.9 10.3 %collective-permute-done.18 = f32[2,256,1]{2,1,0:T(8,128)S(1)} collective-permute-done((f32[2,256,1]{2,1,0:T(8,128)S(1)}, f32[2,256,1]{2,1,0:T(8,128)S(1)}, u32[]{:S(2)}, u32[]{:S(2)}) %collective-permute-start.18) | collective-permute-done | bytes 2080 | tf_op jit(solution)/shard_map/ppermute | solution.py:16
  368.2 2.1 fusion.30
  (128 shorter events, 13.0 us)
Async XLA Ops:
  0.6 1.8 copy-start.32
  2.5 12.4 %collective-permute-start = (f32[3,256,1]{2,1,0:T(8,128)S(1)}, f32[3,256,1]{2,1,0:T(8,128)S(1)}, u32[]{:S(2)}, u32[]{:S(2)}) collective-permute-start(f32[3,256,1]{2,1,0:T(8,128)S(1)} %pad_maximum_fusion.15), channel_id=1, source_target_pairs={{1,0},{2,1},{3,2},{4,3},{5,4},{6,5},{7,6},{8,7},{9,8},{10,9},{11,1... | collective-permute-start | bytes 9224 | tf_op jit(solution)/shard_map/ppermute | solution.py:16
  7.2 7.8 %collective-permute-start.1 = (f32[3,1,1024]{2,1,0:T(1,128)S(1)}, f32[3,1,1024]{2,1,0:T(1,128)S(1)}, u32[]{:S(2)}, u32[]{:S(2)}) collective-permute-start(f32[3,1,1024]{2,1,0:T(1,128)S(1)} %pad_maximum_fusion.16), channel_id=1, source_target_pairs={{16,0},{32,16},{48,32},{64,48},{80,64},{96,80},{112,96},{17,1},{33... | collective-permute-start | bytes 36872 | tf_op jit(solution)/shard_map/ppermute | solution.py:16
  11.2 3.8 %copy-start.33 = (s32[256,1024]{1,0:T(8,128)S(1)}, s32[256,1024]{1,0:T(8,128)}, u32[]{:S(2)}) copy-start(s32[256,1024]{1,0:T(8,128)} %param.7) | copy-start | bytes 3145732
  11.5 5.0 %copy-start.19 = (f32[256,1024]{1,0:T(8,128)S(1)}, f32[256,1024]{1,0:T(8,128)}, u32[]{:S(2)}) copy-start(f32[256,1024]{1,0:T(8,128)} %param.9) | copy-start | bytes 3145732
  11.6 5.0 %copy-start.21 = (f32[256,1024]{1,0:T(8,128)S(1)}, f32[256,1024]{1,0:T(8,128)}, u32[]{:S(2)}) copy-start(f32[256,1024]{1,0:T(8,128)} %param.8) | copy-start | bytes 3145732
  16.5 25.9 %copy-start.7 = (f32[1,256,1024]{2,1,0:T(8,128)}, f32[1,256,1024]{2,1,0:T(8,128)S(1)}, u32[]{:S(2)}) copy-start(f32[1,256,1024]{2,1,0:T(8,128)S(1)} %get-tuple-element.24) | copy-start | bytes 3145732
  16.5 25.9 %copy-start.13 = (f32[1,256,1024]{2,1,0:T(8,128)}, f32[1,256,1024]{2,1,0:T(8,128)S(1)}, u32[]{:S(2)}) copy-start(f32[1,256,1024]{2,1,0:T(8,128)S(1)} %get-tuple-element.20) | copy-start | bytes 3145732
  16.5 25.9 %copy-start.15 = (f32[1,256,1024]{2,1,0:T(8,128)}, f32[1,256,1024]{2,1,0:T(8,128)S(1)}, u32[]{:S(2)}) copy-start(f32[1,256,1024]{2,1,0:T(8,128)S(1)} %get-tuple-element.23) | copy-start | bytes 3145732
  16.5 51.5 %copy-start.1 = (f32[1,256,1024]{2,1,0:T(8,128)}, f32[1,256,1024]{2,1,0:T(8,128)S(1)}, u32[]{:S(2)}) copy-start(f32[1,256,1024]{2,1,0:T(8,128)S(1)} %get-tuple-element.21) | copy-start | bytes 3145732
  16.5 51.5 %copy-start.4 = (f32[1,256,1024]{2,1,0:T(8,128)}, f32[1,256,1024]{2,1,0:T(8,128)S(1)}, u32[]{:S(2)}) copy-start(f32[1,256,1024]{2,1,0:T(8,128)S(1)} %get-tuple-element.22) | copy-start | bytes 3145732
  17.6 15.9 %collective-permute-start.3 = (f32[2,1,1024]{2,1,0:T(1,128)S(1)}, f32[2,1,1024]{2,1,0:T(1,128)S(1)}, u32[]{:S(2)}, u32[]{:S(2)}) collective-permute-start(f32[2,1,1024]{2,1,0:T(1,128)S(1)} %slice.280), channel_id=1, source_target_pairs={{0,16},{16,32},{32,48},{48,64},{64,80},{80,96},{96,112},{1,17},{17... | collective-permute-start | bytes 24584 | tf_op jit(solution)/shard_map/ppermute | solution.py:16
  22.7 10.8 %collective-permute-start.2 = (f32[2,256,1]{2,1,0:T(8,128)S(1)}, f32[2,256,1]{2,1,0:T(8,128)S(1)}, u32[]{:S(2)}, u32[]{:S(2)}) collective-permute-start(f32[2,256,1]{2,1,0:T(8,128)S(1)} %slice.277), channel_id=1, source_target_pairs={{0,1},{1,2},{2,3},{3,4},{4,5},{5,6},{6,7},{7,8},{8,9},{9,10},{10,1... | collective-permute-start | bytes 6152 | tf_op jit(solution)/shard_map/ppermute | solution.py:16
  34.1 7.7 %collective-permute-start.5 = (f32[1,1,1024]{2,1,0:T(1,128)S(1)}, f32[1,1,1024]{2,1,0:T(1,128)S(1)}, u32[]{:S(2)}, u32[]{:S(2)}) collective-permute-start(f32[1,1,1024]{2,1,0:T(1,128)S(1)} %slice.285), channel_id=1, source_target_pairs={{16,0},{32,16},{48,32},{64,48},{80,64},{96,80},{112,96},{17,1},{33... | collective-permute-start | bytes 12296 | tf_op jit(solution)/shard_map/ppermute | solution.py:16
  36.0 5.8 %collective-permute-start.4 = (f32[1,256,1]{2,1,0:T(8,128)S(1)}, f32[1,256,1]{2,1,0:T(8,128)S(1)}, u32[]{:S(2)}, u32[]{:S(2)}) collective-permute-start(f32[1,256,1]{2,1,0:T(8,128)S(1)} %slice.283), channel_id=1, source_target_pairs={{1,0},{2,1},{3,2},{4,3},{5,4},{6,5},{7,6},{8,7},{9,8},{10,9},{11,1... | collective-permute-start | bytes 3080 | tf_op jit(solution)/shard_map/ppermute | solution.py:16
  43.7 15.7 %collective-permute-start.7 = (f32[2,1,1024]{2,1,0:T(1,128)S(1)}, f32[2,1,1024]{2,1,0:T(1,128)S(1)}, u32[]{:S(2)}, u32[]{:S(2)}) collective-permute-start(f32[2,1,1024]{2,1,0:T(1,128)S(1)} %slice.290), channel_id=1, source_target_pairs={{0,16},{16,32},{32,48},{48,64},{64,80},{80,96},{96,112},{1,17},{17... | collective-permute-start | bytes 24584 | tf_op jit(solution)/shard_map/ppermute | solution.py:16
  49.9 9.5 %collective-permute-start.6 = (f32[2,256,1]{2,1,0:T(8,128)S(1)}, f32[2,256,1]{2,1,0:T(8,128)S(1)}, u32[]{:S(2)}, u32[]{:S(2)}) collective-permute-start(f32[2,256,1]{2,1,0:T(8,128)S(1)} %slice.287), channel_id=1, source_target_pairs={{0,1},{1,2},{2,3},{3,4},{4,5},{5,6},{6,7},{7,8},{8,9},{9,10},{10,1... | collective-permute-start | bytes 6152 | tf_op jit(solution)/shard_map/ppermute | solution.py:16
  60.0 2.0 copy-start.28
  60.0 7.7 %collective-permute-start.9 = (f32[1,1,1024]{2,1,0:T(1,128)S(1)}, f32[1,1,1024]{2,1,0:T(1,128)S(1)}, u32[]{:S(2)}, u32[]{:S(2)}) collective-permute-start(f32[1,1,1024]{2,1,0:T(1,128)S(1)} %slice.295), channel_id=1, source_target_pairs={{16,0},{32,16},{48,32},{64,48},{80,64},{96,80},{112,96},{17,1},{33... | collective-permute-start | bytes 12296 | tf_op jit(solution)/shard_map/ppermute | solution.py:16
  62.0 5.7 %collective-permute-start.8 = (f32[1,256,1]{2,1,0:T(8,128)S(1)}, f32[1,256,1]{2,1,0:T(8,128)S(1)}, u32[]{:S(2)}, u32[]{:S(2)}) collective-permute-start(f32[1,256,1]{2,1,0:T(8,128)S(1)} %slice.293), channel_id=1, source_target_pairs={{1,0},{2,1},{3,2},{4,3},{5,4},{6,5},{7,6},{8,7},{9,8},{10,9},{11,1... | collective-permute-start | bytes 3080 | tf_op jit(solution)/shard_map/ppermute | solution.py:16
  65.4 1.7 copy-start.29
  67.2 1.7 copy-start.8
  67.2 2.0 copy-start.14
  67.2 2.3 copy-start.16
  67.2 2.7 copy-start.20
  67.2 2.9 copy-start.22
  150.1 14.1 %collective-permute-start.11 = (f32[2,1,1024]{2,1,0:T(1,128)S(1)}, f32[2,1,1024]{2,1,0:T(1,128)S(1)}, u32[]{:S(2)}, u32[]{:S(2)}) collective-permute-start(f32[2,1,1024]{2,1,0:T(1,128)S(1)} %slice.300), channel_id=1, source_target_pairs={{0,16},{16,32},{32,48},{48,64},{64,80},{80,96},{96,112},{1,17},{17... | collective-permute-start | bytes 24584 | tf_op jit(solution)/shard_map/ppermute | solution.py:16
  152.5 11.7 %collective-permute-start.10 = (f32[2,256,1]{2,1,0:T(8,128)S(1)}, f32[2,256,1]{2,1,0:T(8,128)S(1)}, u32[]{:S(2)}, u32[]{:S(2)}) collective-permute-start(f32[2,256,1]{2,1,0:T(8,128)S(1)} %slice.297), channel_id=1, source_target_pairs={{0,1},{1,2},{2,3},{3,4},{4,5},{5,6},{6,7},{7,8},{8,9},{9,10},{10,1... | collective-permute-start | bytes 6152 | tf_op jit(solution)/shard_map/ppermute | solution.py:16
  164.7 3.0 copy-start.30
  164.8 10.1 %collective-permute-start.13 = (f32[1,1,1024]{2,1,0:T(1,128)S(1)}, f32[1,1,1024]{2,1,0:T(1,128)S(1)}, u32[]{:S(2)}, u32[]{:S(2)}) collective-permute-start(f32[1,1,1024]{2,1,0:T(1,128)S(1)} %slice.305), channel_id=1, source_target_pairs={{16,0},{32,16},{48,32},{64,48},{80,64},{96,80},{112,96},{17,1},{33... | collective-permute-start | bytes 12296 | tf_op jit(solution)/shard_map/ppermute | solution.py:16
  167.7 7.1 %collective-permute-start.12 = (f32[1,256,1]{2,1,0:T(8,128)S(1)}, f32[1,256,1]{2,1,0:T(8,128)S(1)}, u32[]{:S(2)}, u32[]{:S(2)}) collective-permute-start(f32[1,256,1]{2,1,0:T(8,128)S(1)} %slice.303), channel_id=1, source_target_pairs={{1,0},{2,1},{3,2},{4,3},{5,4},{6,5},{7,6},{8,7},{9,8},{10,9},{11,1... | collective-permute-start | bytes 3080 | tf_op jit(solution)/shard_map/ppermute | solution.py:16
  171.4 3.8 %copy-start.2 = (f32[1,256,1024]{2,1,0:T(8,128)S(1)}, f32[1,256,1024]{2,1,0:T(8,128)}, u32[]{:S(2)}) copy-start(f32[1,256,1024]{2,1,0:T(8,128)} %copy-done.1) | copy-start | bytes 3145732
  171.4 3.8 %copy-start.5 = (f32[1,256,1024]{2,1,0:T(8,128)S(1)}, f32[1,256,1024]{2,1,0:T(8,128)}, u32[]{:S(2)}) copy-start(f32[1,256,1024]{2,1,0:T(8,128)} %copy-done.4) | copy-start | bytes 3145732
  171.4 3.8 %copy-start.9 = (f32[1,256,1024]{2,1,0:T(8,128)S(1)}, f32[1,256,1024]{2,1,0:T(8,128)}, u32[]{:S(2)}) copy-start(f32[1,256,1024]{2,1,0:T(8,128)} %copy-done.7) | copy-start | bytes 3145732
  171.4 3.8 %copy-start.11 = (f32[2,256,1024]{2,1,0:T(8,128)S(1)}, f32[2,256,1024]{2,1,0:T(8,128)}, u32[]{:S(2)}) copy-start(f32[2,256,1024]{2,1,0:T(8,128)} %get-tuple-element.15) | copy-start | bytes 6291460
  250.8 25.0 %copy-start = (f32[2,256,1024]{2,1,0:T(8,128)}, f32[2,256,1024]{2,1,0:T(8,128)S(1)}, u32[]{:S(2)}) copy-start(f32[2,256,1024]{2,1,0:T(8,128)S(1)} %multiply_subtract_fusion) | copy-start | bytes 6291460
  250.8 14.0 %collective-permute-start.15 = (f32[2,1,1024]{2,1,0:T(1,128)S(1)}, f32[2,1,1024]{2,1,0:T(1,128)S(1)}, u32[]{:S(2)}, u32[]{:S(2)}) collective-permute-start(f32[2,1,1024]{2,1,0:T(1,128)S(1)} %slice.310), channel_id=1, source_target_pairs={{0,16},{16,32},{32,48},{48,64},{64,80},{80,96},{96,112},{1,17},{17... | collective-permute-start | bytes 24584 | tf_op jit(solution)/shard_map/ppermute | solution.py:16
  253.1 11.6 %collective-permute-start.14 = (f32[2,256,1]{2,1,0:T(8,128)S(1)}, f32[2,256,1]{2,1,0:T(8,128)S(1)}, u32[]{:S(2)}, u32[]{:S(2)}) collective-permute-start(f32[2,256,1]{2,1,0:T(8,128)S(1)} %slice.307), channel_id=1, source_target_pairs={{0,1},{1,2},{2,3},{3,4},{4,5},{5,6},{6,7},{7,8},{8,9},{9,10},{10,1... | collective-permute-start | bytes 6152 | tf_op jit(solution)/shard_map/ppermute | solution.py:16
  265.3 10.1 %collective-permute-start.17 = (f32[1,1,1024]{2,1,0:T(1,128)S(1)}, f32[1,1,1024]{2,1,0:T(1,128)S(1)}, u32[]{:S(2)}, u32[]{:S(2)}) collective-permute-start(f32[1,1,1024]{2,1,0:T(1,128)S(1)} %slice.315), channel_id=1, source_target_pairs={{16,0},{32,16},{48,32},{64,48},{80,64},{96,80},{112,96},{17,1},{33... | collective-permute-start | bytes 12296 | tf_op jit(solution)/shard_map/ppermute | solution.py:16
  268.3 7.1 %collective-permute-start.16 = (f32[1,256,1]{2,1,0:T(8,128)S(1)}, f32[1,256,1]{2,1,0:T(8,128)S(1)}, u32[]{:S(2)}, u32[]{:S(2)}) collective-permute-start(f32[1,256,1]{2,1,0:T(8,128)S(1)} %slice.313), channel_id=1, source_target_pairs={{1,0},{2,1},{3,2},{4,3},{5,4},{6,5},{7,6},{8,7},{9,8},{10,9},{11,1... | collective-permute-start | bytes 3080 | tf_op jit(solution)/shard_map/ppermute | solution.py:16
  270.6 5.2 %copy-start.27 = (f32[2,256,1024]{2,1,0:T(8,128)S(1)}, f32[2,256,1024]{2,1,0:T(8,128)}, u32[]{:S(2)}) copy-start(f32[2,256,1024]{2,1,0:T(8,128)} %get-tuple-element.14) | copy-start | bytes 6291460
  270.8 5.0 %copy-start.3 = (f32[1,256,1024]{2,1,0:T(8,128)S(1)}, f32[1,256,1024]{2,1,0:T(8,128)}, u32[]{:S(2)}) copy-start(f32[1,256,1024]{2,1,0:T(8,128)} %copy-done.1) | copy-start | bytes 3145732
  270.8 5.0 %copy-start.6 = (f32[1,256,1024]{2,1,0:T(8,128)S(1)}, f32[1,256,1024]{2,1,0:T(8,128)}, u32[]{:S(2)}) copy-start(f32[1,256,1024]{2,1,0:T(8,128)} %copy-done.4) | copy-start | bytes 3145732
  270.8 5.0 %copy-start.10 = (f32[1,256,1024]{2,1,0:T(8,128)S(1)}, f32[1,256,1024]{2,1,0:T(8,128)}, u32[]{:S(2)}) copy-start(f32[1,256,1024]{2,1,0:T(8,128)} %copy-done.7) | copy-start | bytes 3145732
  270.8 5.0 %copy-start.12 = (f32[2,256,1024]{2,1,0:T(8,128)S(1)}, f32[2,256,1024]{2,1,0:T(8,128)}, u32[]{:S(2)}) copy-start(f32[2,256,1024]{2,1,0:T(8,128)} %get-tuple-element.15) | copy-start | bytes 6291460
  347.7 20.6 %copy-start.18 = (f32[256,1024]{1,0:T(8,128)S(1)}, f32[256,1024]{1,0:T(8,128)}, u32[]{:S(2)}) copy-start(f32[256,1024]{1,0:T(8,128)} %param.5) | copy-start | bytes 3145732
  353.0 15.2 %collective-permute-start.19 = (f32[2,1,1024]{2,1,0:T(1,128)S(1)}, f32[2,1,1024]{2,1,0:T(1,128)S(1)}, u32[]{:S(2)}, u32[]{:S(2)}) collective-permute-start(f32[2,1,1024]{2,1,0:T(1,128)S(1)} %slice.320), channel_id=1, source_target_pairs={{0,16},{16,32},{32,48},{48,64},{64,80},{80,96},{96,112},{1,17},{17... | collective-permute-start | bytes 24584 | tf_op jit(solution)/shard_map/ppermute | solution.py:16
  355.9 12.3 %collective-permute-start.18 = (f32[2,256,1]{2,1,0:T(8,128)S(1)}, f32[2,256,1]{2,1,0:T(8,128)S(1)}, u32[]{:S(2)}, u32[]{:S(2)}) collective-permute-start(f32[2,256,1]{2,1,0:T(8,128)S(1)} %slice.317), channel_id=1, source_target_pairs={{0,1},{1,2},{2,3},{3,4},{4,5},{5,6},{6,7},{7,8},{8,9},{9,10},{10,1... | collective-permute-start | bytes 6152 | tf_op jit(solution)/shard_map/ppermute | solution.py:16
  (6 other events, 8.6 us)
